TPU v7x, 32 devices: a whole 2x2x4 slice. The times are simulated.
32 devices in a mesh: pole: 4 (over y, x), row: 8 (over z, core).
Axes of the slice: x: 2, y: 2, z: 4, core: 2. Of those that a mesh axis runs over, the one named last changes fastest.
Arguments:
- basis: bfloat16 [32768, 128], P('row'), may hold values from -24 to 24
- inverses: bfloat16 [4, 64, 512, 512], P('pole', 'row'), may hold values from -1.5 to 1.5
- lower: bfloat16 [64, 512, 512], P('row'), may hold values from -0.03955078 to 0.03955078
- upper: bfloat16 [64, 512, 512], P('row'), may hold values from -0.03955078 to 0.03955078
- pole_weights: float32 [4], P('pole'), may hold values from 0.5 to 1.5
Outputs:
- new_basis: float32 [32768, 128], P(('row', 'pole'))
All inputs are finite; a program needn't handle non-finite values.
Results may differ from a plain program's by a relative error of at most 0.003.
Values may be sent and summed in bfloat16 or wider, within the bound.
A program may use at most 64 MiB of HBM per device.

v0:
```python
import jax
import jax.numpy as jnp
from jax import lax
from jax.sharding import PartitionSpec as P

SWEEPS = 4


def padded_2(value, sides, width):
    for axis, dim in sides:
        peers, length = (lax.axis_size(axis), value.shape[dim])
        up = [(i, (i + 1) % peers) for i in range(peers - 1)]
        down = [(j, i) for i, j in up]
        last = lax.slice_in_dim(value, length - width, length, axis=dim)
        initial = lax.slice_in_dim(value, 0, width, axis=dim)
        before = lax.ppermute(last, axis, up)
        after = lax.ppermute(initial, axis, down)
        value = jnp.concatenate([before, value, after], axis=dim)
    return value


def shards(basis, inverses, lower, upper, pole_weights):
    rows, width = basis.shape
    count = inverses.shape[1]
    size = inverses.shape[-1]
    inverse = inverses[0]
    blocks = basis.reshape(count, size, width)
    state = jnp.einsum("bij,bjk->bik", inverse, blocks, preferred_element_type=jnp.float32).astype(
        jnp.bfloat16
    )
    for sweep in range(SWEEPS):
        padded = padded_2(state.reshape(rows, width), (("row", 0),), size)
        padded = padded.reshape(count + 2, size, width)
        rhs = blocks.astype(jnp.float32)
        rhs = rhs + jnp.einsum(
            "bij,bjk->bik", lower, padded[:-2], preferred_element_type=jnp.float32
        )
        rhs = rhs + jnp.einsum(
            "bij,bjk->bik", upper, padded[2:], preferred_element_type=jnp.float32
        )
        state = jnp.einsum(
            "bij,bjk->bik", inverse, rhs.astype(jnp.bfloat16), preferred_element_type=jnp.float32
        ).astype(jnp.bfloat16)
    weighted = pole_weights[0] * state.reshape(rows, width).astype(jnp.float32)
    total_rows = rows * lax.axis_size("row")
    filtered = lax.psum(weighted, "pole")
    share = rows // lax.axis_size("pole")
    mine = lax.dynamic_slice_in_dim(filtered, lax.axis_index("pole") * share, share, 0)
    partial_gram = jnp.dot(filtered.T, filtered, precision=lax.Precision.HIGHEST)
    gram = lax.psum(partial_gram, "row")
    gram = gram / total_rows
    factor = jnp.linalg.cholesky(gram)
    solved = jax.scipy.linalg.solve_triangular(factor, mine.T, lower=True)
    return solved.T


def solution(mesh):
    return jax.shard_map(
        shards,
        mesh=mesh,
        in_specs=(
            P("row", None),
            P("pole", "row", None, None),
            P("row", None, None),
            P("row", None, None),
            P("pole"),
        ),
        out_specs=P(("row", "pole"), None),
        check_vma=False,
    )
```

profile of v0, /device:TPU:0, one launch (start us, length us, event | category | flops | bytes accessed | tf_op | source)
XLA Modules:
  0.0 268.5 jit_solution(1977090597358284194)
XLA Ops:
  6.5 3.8 %fusion.18 = bf16[8,512,128]{2,1,0:T(8,128)(2,1)S(1)} fusion(bf16[8,512,128]{2,1,0:T(8,128)(2,1)} %bitcast.142, bf16[1,8,512,512]{3,2,1,0:T(8,128)(2,1)} %param.6), kind=kOutput, calls=%fused_computation.23 | convolution fusion | flops 537395200 | bytes 6291456 | tf_op jit(solution)/shard_map/bij,bjk->bik/dot_general | solution.py:28
  10.4 2.4 collective-permute-start
  12.8 1.3 collective-permute-start.1
  14.1 0.5 copy.15
  14.7 3.7 %collective-permute-done.1 = bf16[512,128]{1,0:T(8,128)(2,1)} collective-permute-done((bf16[512,128]{1,0:T(8,128)(2,1)S(1)}, bf16[512,128]{1,0:T(8,128)(2,1)}, u32[]{:S(2)}, u32[]{:S(2)}) %collective-permute-start.1) | collective-permute-done | bytes 131104 | tf_op jit(solution)/shard_map/ppermute | solution.py:17
  18.4 2.0 pad_maximum_fusion.6
  20.4 3.7 %fusion.50 = f32[8,128,512]{2,1,0:T(8,128)S(1)} fusion(bf16[8,512,128]{2,1,0:T(8,128)(2,1)S(1)} %bitcast.131, bf16[8,512,512]{2,1,0:T(8,128)(2,1)} %param.7), kind=kOutput, calls=%fused_computation.60 | convolution fusion | flops 536870912 | bytes 7340032 | tf_op jit(solution)/shard_map/bij,bjk->bik/dot_general | solution.py:35
  24.1 7.6 %fusion.41 = bf16[8,512,128]{1,2,0:T(8,128)(2,1)} fusion(bf16[1,8,512,512]{3,2,1,0:T(8,128)(2,1)} %param.6, bf16[8,512,128]{1,2,0:T(8,128)(2,1)S(1)} %copy.15, f32[8,128,512]{2,1,0:T(8,128)S(1)} %fusion.50, bf16[8,512,128]{2,1,0:T(8,128)(2,1)} %bitcast.138, bf16[8,512,512]{2,1,0:T(8,128)(2,1)} %param.8), kind=kOutput, calls=%fused_computation.30 | convolution fusion | flops 1076363264 | bytes 13631488 | tf_op jit(solution)/shard_map/bij,bjk->bik/dot_general | solution.py:41
  31.7 1.0 slice_bitcast_fusion.4
  32.7 5.4 %collective-permute-start.2 = (bf16[512,128]{0,1:T(8,128)(2,1)S(1)}, bf16[512,128]{0,1:T(8,128)(2,1)S(1)}, u32[]{:S(2)}, u32[]{:S(2)}) collective-permute-start(bf16[512,128]{0,1:T(8,128)(2,1)S(1)} %get-tuple-element.16), channel_id=1, source_target_pairs={{0,1},{1,2},{2,3},{3,4},{4,5},{5,6},{6,7},{8,9},{9,10},{10,11},{11... | collective-permute-start | bytes 393224 | tf_op jit(solution)/shard_map/ppermute | solution.py:16
  38.1 1.3 collective-permute-start.3
  39.4 1.6 copy.16
  41.1 0.1 copy.17
  41.2 0.2 collective-permute-done.3
  41.4 0.1 copy.18
  41.5 1.1 pad_maximum_fusion.4
  42.6 3.7 %fusion.51 = f32[8,128,512]{2,1,0:T(8,128)S(1)} fusion(bf16[8,512,128]{2,1,0:T(8,128)(2,1)S(1)} %bitcast.132, bf16[8,512,512]{2,1,0:T(8,128)(2,1)} %param.7), kind=kOutput, calls=%fused_computation.61 | convolution fusion | flops 536870912 | bytes 7340032 | tf_op jit(solution)/shard_map/bij,bjk->bik/dot_general | solution.py:35
  46.3 7.6 %fusion.38 = bf16[8,512,128]{1,2,0:T(8,128)(2,1)} fusion(bf16[1,8,512,512]{3,2,1,0:T(8,128)(2,1)} %param.6, bf16[8,512,128]{1,2,0:T(8,128)(2,1)S(1)} %copy.15, f32[8,128,512]{2,1,0:T(8,128)S(1)} %fusion.51, bf16[8,512,128]{2,1,0:T(8,128)(2,1)} %bitcast.139, bf16[8,512,512]{2,1,0:T(8,128)(2,1)} %param.8), kind=kOutput, calls=%fused_computation.29 | convolution fusion | flops 1076363264 | bytes 13631488 | tf_op jit(solution)/shard_map/bij,bjk->bik/dot_general | solution.py:41
  54.0 1.0 slice_bitcast_fusion.2
  55.0 5.0 %collective-permute-start.4 = (bf16[512,128]{0,1:T(8,128)(2,1)S(1)}, bf16[512,128]{0,1:T(8,128)(2,1)S(1)}, u32[]{:S(2)}, u32[]{:S(2)}) collective-permute-start(bf16[512,128]{0,1:T(8,128)(2,1)S(1)} %get-tuple-element.12), channel_id=1, source_target_pairs={{0,1},{1,2},{2,3},{3,4},{4,5},{5,6},{6,7},{8,9},{9,10},{10,11},{11... | collective-permute-start | bytes 393224 | tf_op jit(solution)/shard_map/ppermute | solution.py:16
  59.9 1.3 collective-permute-start.5
  61.2 1.6 copy.19
  62.9 0.1 copy.20
  63.0 0.2 collective-permute-done.5
  63.2 0.1 copy.21
  63.3 1.1 pad_maximum_fusion.2
  64.4 3.7 %fusion.52 = f32[8,128,512]{2,1,0:T(8,128)S(1)} fusion(bf16[8,512,128]{2,1,0:T(8,128)(2,1)S(1)} %bitcast.133, bf16[8,512,512]{2,1,0:T(8,128)(2,1)} %param.7), kind=kOutput, calls=%fused_computation.62 | convolution fusion | flops 536870912 | bytes 7340032 | tf_op jit(solution)/shard_map/bij,bjk->bik/dot_general | solution.py:35
  68.1 7.6 %fusion.35 = bf16[8,512,128]{1,2,0:T(8,128)(2,1)} fusion(bf16[1,8,512,512]{3,2,1,0:T(8,128)(2,1)} %param.6, bf16[8,512,128]{1,2,0:T(8,128)(2,1)S(1)} %copy.15, f32[8,128,512]{2,1,0:T(8,128)S(1)} %fusion.52, bf16[8,512,128]{2,1,0:T(8,128)(2,1)} %bitcast.140, bf16[8,512,512]{2,1,0:T(8,128)(2,1)} %param.8), kind=kOutput, calls=%fused_computation.28 | convolution fusion | flops 1076363264 | bytes 13631488 | tf_op jit(solution)/shard_map/bij,bjk->bik/dot_general | solution.py:41
  75.7 1.0 slice_bitcast_fusion
  76.7 5.0 %collective-permute-start.6 = (bf16[512,128]{0,1:T(8,128)(2,1)S(1)}, bf16[512,128]{0,1:T(8,128)(2,1)S(1)}, u32[]{:S(2)}, u32[]{:S(2)}) collective-permute-start(bf16[512,128]{0,1:T(8,128)(2,1)S(1)} %get-tuple-element.8), channel_id=1, source_target_pairs={{0,1},{1,2},{2,3},{3,4},{4,5},{5,6},{6,7},{8,9},{9,10},{10,11},{11... | collective-permute-start | bytes 393224 | tf_op jit(solution)/shard_map/ppermute | solution.py:16
  81.7 1.5 collective-permute-start.7
  83.8 1.6 copy.22
  85.5 0.1 copy.23
  85.6 0.1 copy.24
  85.7 1.1 pad_maximum_fusion
  86.9 3.7 %fusion.53 = f32[8,128,512]{2,1,0:T(8,128)S(1)} fusion(bf16[8,512,128]{2,1,0:T(8,128)(2,1)S(1)} %bitcast.134, bf16[8,512,512]{2,1,0:T(8,128)(2,1)} %param.7), kind=kOutput, calls=%fused_computation.63 | convolution fusion | flops 536870912 | bytes 7340032 | tf_op jit(solution)/shard_map/bij,bjk->bik/dot_general | solution.py:35
  90.6 8.0 %multiply_bitcast_fusion = f32[8,512,128]{1,2,0:T(8,128)} fusion(bf16[1,8,512,512]{3,2,1,0:T(8,128)(2,1)} %param.6, bf16[8,512,128]{1,2,0:T(8,128)(2,1)S(1)} %copy.15, f32[8,128,512]{2,1,0:T(8,128)S(1)} %fusion.53, bf16[8,512,128]{2,1,0:T(8,128)(2,1)} %bitcast.130, bf16[8,512,512]{2,1,0:T(8,128)(2,1)} %param.8, f32[]{:T(128)} %bitcast.128), kind=kOutput, calls=%fused_computation.22 | convolution fusion | flops 1077411840 | bytes 14680068 | tf_op jit(solution)/shard_map/bij,bjk->bik/dot_general | solution.py:41
  98.5 2.9 %copy.25 = f32[8,512,128]{2,1,0:T(8,128)} copy(f32[8,512,128]{1,2,0:T(8,128)} %multiply_bitcast_fusion) | data formatting | bytes 4194304 | tf_op jit(solution)/shard_map/mul | solution.py:44
  101.5 71.8 %all-reduce.3.cloned.1.call-done = f32[4096,128]{1,0:T(8,128)} async-done(((f32[4096,128]{1,0:T(8,128)}), f32[4096,128]{1,0:T(8,128)}) %all-reduce.3.cloned.1.call-update) | async-done | bytes 2097168 | tf_op jit(solution)/shard_map/psum | solution.py:46
  173.4 6.3 %fusion.54 = f32[128,128]{0,1:T(8,128)} fusion(f32[4096,128]{1,0:T(8,128)} %all-reduce.3.cloned.1.call-done), kind=kOutput, calls=%fused_computation.64 | convolution fusion | flops 805306368 | bytes 2162688 | tf_op jit(solution)/shard_map/dot_general | solution.py:49
  179.7 54.8 %all-reduce.5.cloned.1.call-done = f32[128,128]{0,1:T(8,128)} async-done(((f32[128,128]{0,1:T(8,128)}), f32[128,128]{0,1:T(8,128)}) %all-reduce.5.cloned.1.call-update) | async-done | bytes 65552 | tf_op jit(solution)/shard_map/psum | solution.py:50
  234.5 0.8 broadcast_multiply_fusion
  235.5 0.9 fusion.48
  236.3 11.7 %cholesky.16 = f32[128,128]{1,0:T(8,128)S(1)} custom-call(f32[128,128]{1,0:T(8,128)S(1)} %fusion.48), custom_call_target="Cholesky" | custom-call | tf_op jit(solution)/shard_map/jit(cholesky)/cholesky | solution.py:52
  248.1 0.6 compare_reduce_fusion
  248.7 0.7 fusion.46
  249.4 9.8 %custom-call.7 = f32[1,128,128]{1,2,0:T(8,128)S(1)} custom-call(f32[1,128,128]{2,1,0:T(8,128)S(1)} %fusion.46), custom_call_target="InvertDiagBlocksLowerTriangular" | custom-call | tf_op jit(solution)/shard_map/jit(_solve_triangular)/triangular_solve | solution.py:53
  259.2 2.4 fusion.44
  (14 shorter events, 0.2 us)
Async XLA Ops:
  6.5 166.8 %all-reduce.3.cloned.1.call-start = ((), (), s32[]{:S(2)}) async-start(), calls=%async_computation | async-start | bytes 4194304 | tf_op jit(solution)/shard_map/psum | solution.py:46
  6.5 7.6 %copy-start = (bf16[4096,128]{1,0:T(8,128)(2,1)S(1)}, bf16[4096,128]{1,0:T(8,128)(2,1)}, u32[]{:S(2)}) copy-start(bf16[4096,128]{1,0:T(8,128)(2,1)} %param.5) | copy-start | bytes 3145732
  10.4 4.3 %collective-permute-start = (bf16[512,128]{1,0:T(8,128)(2,1)S(1)}, bf16[512,128]{1,0:T(8,128)(2,1)S(1)}, u32[]{:S(2)}, u32[]{:S(2)}) collective-permute-start(bf16[512,128]{1,0:T(8,128)(2,1)S(1)} %get-tuple-element.20), channel_id=1, source_target_pairs={{0,1},{1,2},{2,3},{3,4},{4,5},{5,6},{6,7},{8,9},{9,10},{10,11},{11... | collective-permute-start | bytes 393224 | tf_op jit(solution)/shard_map/ppermute | solution.py:16
  12.8 5.5 %collective-permute-start.1 = (bf16[512,128]{1,0:T(8,128)(2,1)S(1)}, bf16[512,128]{1,0:T(8,128)(2,1)}, u32[]{:S(2)}, u32[]{:S(2)}) collective-permute-start(bf16[512,128]{1,0:T(8,128)(2,1)S(1)} %get-tuple-element.19), channel_id=1, source_target_pairs={{1,0},{2,1},{3,2},{4,3},{5,4},{6,5},{7,6},{9,8},{10,9},{11,10},{12... | collective-permute-start | bytes 393224 | tf_op jit(solution)/shard_map/ppermute | solution.py:17
  32.7 8.4 %collective-permute-start.2 = (bf16[512,128]{0,1:T(8,128)(2,1)S(1)}, bf16[512,128]{0,1:T(8,128)(2,1)S(1)}, u32[]{:S(2)}, u32[]{:S(2)}) collective-permute-start(bf16[512,128]{0,1:T(8,128)(2,1)S(1)} %get-tuple-element.16), channel_id=1, source_target_pairs={{0,1},{1,2},{2,3},{3,4},{4,5},{5,6},{6,7},{8,9},{9,10},{10,11},{11... | collective-permute-start | bytes 393224 | tf_op jit(solution)/shard_map/ppermute | solution.py:16
  38.1 3.2 %collective-permute-start.3 = (bf16[512,128]{0,1:T(8,128)(2,1)S(1)}, bf16[512,128]{0,1:T(8,128)(2,1)S(1)}, u32[]{:S(2)}, u32[]{:S(2)}) collective-permute-start(bf16[512,128]{0,1:T(8,128)(2,1)S(1)} %get-tuple-element.15), channel_id=1, source_target_pairs={{1,0},{2,1},{3,2},{4,3},{5,4},{6,5},{7,6},{9,8},{10,9},{11,10},{12... | collective-permute-start | bytes 393224 | tf_op jit(solution)/shard_map/ppermute | solution.py:17
  55.0 7.9 %collective-permute-start.4 = (bf16[512,128]{0,1:T(8,128)(2,1)S(1)}, bf16[512,128]{0,1:T(8,128)(2,1)S(1)}, u32[]{:S(2)}, u32[]{:S(2)}) collective-permute-start(bf16[512,128]{0,1:T(8,128)(2,1)S(1)} %get-tuple-element.12), channel_id=1, source_target_pairs={{0,1},{1,2},{2,3},{3,4},{4,5},{5,6},{6,7},{8,9},{9,10},{10,11},{11... | collective-permute-start | bytes 393224 | tf_op jit(solution)/shard_map/ppermute | solution.py:16
  59.9 3.2 %collective-permute-start.5 = (bf16[512,128]{0,1:T(8,128)(2,1)S(1)}, bf16[512,128]{0,1:T(8,128)(2,1)S(1)}, u32[]{:S(2)}, u32[]{:S(2)}) collective-permute-start(bf16[512,128]{0,1:T(8,128)(2,1)S(1)} %get-tuple-element.11), channel_id=1, source_target_pairs={{1,0},{2,1},{3,2},{4,3},{5,4},{6,5},{7,6},{9,8},{10,9},{11,10},{12... | collective-permute-start | bytes 393224 | tf_op jit(solution)/shard_map/ppermute | solution.py:17
  76.7 8.7 %collective-permute-start.6 = (bf16[512,128]{0,1:T(8,128)(2,1)S(1)}, bf16[512,128]{0,1:T(8,128)(2,1)S(1)}, u32[]{:S(2)}, u32[]{:S(2)}) collective-permute-start(bf16[512,128]{0,1:T(8,128)(2,1)S(1)} %get-tuple-element.8), channel_id=1, source_target_pairs={{0,1},{1,2},{2,3},{3,4},{4,5},{5,6},{6,7},{8,9},{9,10},{10,11},{11... | collective-permute-start | bytes 393224 | tf_op jit(solution)/shard_map/ppermute | solution.py:16
  81.7 3.9 %collective-permute-start.7 = (bf16[512,128]{0,1:T(8,128)(2,1)S(1)}, bf16[512,128]{0,1:T(8,128)(2,1)S(1)}, u32[]{:S(2)}, u32[]{:S(2)}) collective-permute-start(bf16[512,128]{0,1:T(8,128)(2,1)S(1)} %get-tuple-element.7), channel_id=1, source_target_pairs={{1,0},{2,1},{3,2},{4,3},{5,4},{6,5},{7,6},{9,8},{10,9},{11,10},{12... | collective-permute-start | bytes 393224 | tf_op jit(solution)/shard_map/ppermute | solution.py:17
  101.5 133.1 %all-reduce.5.cloned.1.call-start = ((), (), s32[]{:S(2)}) async-start(), calls=%async_computation.1 | async-start | bytes 131072 | tf_op jit(solution)/shard_map/psum | solution.py:50
Sparse Core Ops, SparseCore 0:
  101.6 71.7 all-reduce.2
  179.8 54.6 all-reduce.4
where the time goes:
time: 269 us; the launch traced here: 268 us
  waiting for transfers between devices  131 us (49%)
  matrix products  58.2 us (22%)
  other arithmetic  29.9 us (11%)
  starting transfers between devices  23.2 us (9%)
  between operations  14.3 us (5%)
  local copies, waits for them, and re-layouts  12.1 us (4%)
    psum x1, waiting for transfers between devices, shards(): filtered = lax.psum(weighted, 'pole')  71.8 us
    psum x1, waiting for transfers between devices, shards(): gram = lax.psum(partial_gram, 'row')  54.8 us
    dot_general x4, matrix products, shards(): jnp.einsum('bij,bjk->bik', inverse, rhs.astype(jnp.bfloat16), preferred_e...  30.9 us
    ppermute x4, starting transfers between devices, padded_2(): before = lax.ppermute(last, axis, up)  17.8 us
    dot_general x4, matrix products, shards(): jnp.einsum('bij,bjk->bik', lower, padded[:-2], preferred_element_type=jnp...  14.8 us
    another operation x3, other arithmetic, shards(): factor = jnp.linalg.cholesky(gram)  12.4 us
    another operation x2, other arithmetic, shards(): solved = jax.scipy.linalg.solve_triangular(factor, mine.T, lower=True)  10.5 us
    dot_general x1, matrix products, shards(): jnp.dot(filtered.T, filtered, precision=lax.Precision.HIGHEST)  6.31 us
  transfers between devices with their start and end apart: 10, of which 5 were waited for; matrix products, arithmetic and copies ran while one was open for 2% of the time, Pallas kernels for 0%

commit v1 on v0

--- a/solution.py
+++ b/solution.py
@@ -47,7 +47,7 @@
     share = rows // lax.axis_size("pole")
     mine = lax.dynamic_slice_in_dim(filtered, lax.axis_index("pole") * share, share, 0)
     partial_gram = jnp.dot(filtered.T, filtered, precision=lax.Precision.HIGHEST)
-    gram = lax.psum(partial_gram, "row")
+    gram = jnp.sum(lax.all_gather(partial_gram, "row"), axis=0)
     gram = gram / total_rows
     factor = jnp.linalg.cholesky(gram)
     solved = jax.scipy.linalg.solve_triangular(factor, mine.T, lower=True)

time: 269 us -> 227 us (0.84)
  waiting for transfers between devices: 131 us -> 76 us
  blocking collectives: 0 us -> 15 us
    psum x1 -> x0, waiting for transfers between devices: 54.8 us -> none  [shards(): gram = lax.psum(partial_gram, 'row')]
    all_gather x0 -> x1, blocking collectives: none -> 15 us  [shards(): gram = jnp.sum(lax.all_gather(partial_gram, 'row'), axis=0)]
  transfers between devices with their start and end apart: 10 -> 9, of which waited for: 5 -> 4; matrix products, arithmetic and copies ran while one was open for 2% -> 3% of each run, Pallas kernels for 0% -> 0%
where the time goes in v1:
time: 227 us; the launch traced here: 226 us
  waiting for transfers between devices  76 us (33%)
  matrix products  57.6 us (25%)
  other arithmetic  28.2 us (12%)
  starting transfers between devices  23.1 us (10%)
  blocking collectives  15 us (7%)
  between operations  14.3 us (6%)
  local copies, waits for them, and re-layouts  12 us (5%)
    psum x1, waiting for transfers between devices, shards(): filtered = lax.psum(weighted, 'pole')  71.9 us
    dot_general x4, matrix products, shards(): jnp.einsum('bij,bjk->bik', inverse, rhs.astype(jnp.bfloat16), preferred_e...  31 us
    ppermute x4, starting transfers between devices, padded_2(): before = lax.ppermute(last, axis, up)  17.8 us
    all_gather x1, blocking collectives, shards(): gram = jnp.sum(lax.all_gather(partial_gram, 'row'), axis=0)  15 us
    dot_general x4, matrix products, shards(): jnp.einsum('bij,bjk->bik', lower, padded[:-2], preferred_element_type=jnp...  14.8 us
    another operation x3, other arithmetic, shards(): factor = jnp.linalg.cholesky(gram)  12.4 us
    another operation x2, other arithmetic, shards(): solved = jax.scipy.linalg.solve_triangular(factor, mine.T, lower=True)  10.5 us
    dot_general x1, matrix products, shards(): jnp.dot(filtered.T, filtered, precision=lax.Precision.HIGHEST)  5.66 us
  transfers between devices with their start and end apart: 9, of which 4 were waited for; matrix products, arithmetic and copies ran while one was open for 3% of the time, Pallas kernels for 0%

profile of v1, /device:TPU:0, one launch (start us, length us, event | category | flops | bytes accessed | tf_op | source)
XLA Modules:
  0.0 226.3 jit_solution(10256084464301204904)
XLA Ops:
  6.5 3.8 %fusion.18 = bf16[8,512,128]{2,1,0:T(8,128)(2,1)S(1)} fusion(bf16[8,512,128]{2,1,0:T(8,128)(2,1)} %bitcast.144, bf16[1,8,512,512]{3,2,1,0:T(8,128)(2,1)} %param.6), kind=kOutput, calls=%fused_computation.23 | convolution fusion | flops 537395200 | bytes 6291456 | tf_op jit(solution)/shard_map/bij,bjk->bik/dot_general | solution.py:28
  10.4 2.4 %collective-permute-start = (bf16[512,128]{1,0:T(8,128)(2,1)S(1)}, bf16[512,128]{1,0:T(8,128)(2,1)S(1)}, u32[]{:S(2)}, u32[]{:S(2)}) collective-permute-start(bf16[512,128]{1,0:T(8,128)(2,1)S(1)} %get-tuple-element.20), channel_id=1, source_target_pairs={{0,1},{1,2},{2,3},{3,4},{4,5},{5,6},{6,7},{8,9},{9,10},{10,11},{11... | collective-permute-start | bytes 393224 | tf_op jit(solution)/shard_map/ppermute | solution.py:16
  12.8 1.3 collective-permute-start.1
  14.1 0.5 copy.38
  14.7 3.7 %collective-permute-done.1 = bf16[512,128]{1,0:T(8,128)(2,1)} collective-permute-done((bf16[512,128]{1,0:T(8,128)(2,1)S(1)}, bf16[512,128]{1,0:T(8,128)(2,1)}, u32[]{:S(2)}, u32[]{:S(2)}) %collective-permute-start.1) | collective-permute-done | bytes 131104 | tf_op jit(solution)/shard_map/ppermute | solution.py:17
  18.4 2.0 pad_maximum_fusion.6
  20.4 3.7 %fusion.50 = f32[8,128,512]{2,1,0:T(8,128)S(1)} fusion(bf16[8,512,128]{2,1,0:T(8,128)(2,1)S(1)} %bitcast.132, bf16[8,512,512]{2,1,0:T(8,128)(2,1)} %param.7), kind=kOutput, calls=%fused_computation.59 | convolution fusion | flops 536870912 | bytes 7340032 | tf_op jit(solution)/shard_map/bij,bjk->bik/dot_general | solution.py:35
  24.1 7.7 %fusion.41 = bf16[8,512,128]{1,2,0:T(8,128)(2,1)} fusion(bf16[1,8,512,512]{3,2,1,0:T(8,128)(2,1)} %param.6, bf16[8,512,128]{1,2,0:T(8,128)(2,1)S(1)} %copy.38, f32[8,128,512]{2,1,0:T(8,128)S(1)} %fusion.50, bf16[8,512,128]{2,1,0:T(8,128)(2,1)} %bitcast.139, bf16[8,512,512]{2,1,0:T(8,128)(2,1)} %param.8), kind=kOutput, calls=%fused_computation.30 | convolution fusion | flops 1076363264 | bytes 13631488 | tf_op jit(solution)/shard_map/bij,bjk->bik/dot_general | solution.py:41
  31.7 1.0 slice_bitcast_fusion.4
  32.7 5.4 %collective-permute-start.2 = (bf16[512,128]{0,1:T(8,128)(2,1)S(1)}, bf16[512,128]{0,1:T(8,128)(2,1)S(1)}, u32[]{:S(2)}, u32[]{:S(2)}) collective-permute-start(bf16[512,128]{0,1:T(8,128)(2,1)S(1)} %get-tuple-element.16), channel_id=1, source_target_pairs={{0,1},{1,2},{2,3},{3,4},{4,5},{5,6},{6,7},{8,9},{9,10},{10,11},{11... | collective-permute-start | bytes 393224 | tf_op jit(solution)/shard_map/ppermute | solution.py:16
  38.2 1.3 collective-permute-start.3
  39.5 1.6 copy.41
  41.1 0.1 copy.42
  41.2 0.2 collective-permute-done.3
  41.4 0.1 copy.44
  41.5 1.1 pad_maximum_fusion.4
  42.6 3.7 %fusion.51 = f32[8,128,512]{2,1,0:T(8,128)S(1)} fusion(bf16[8,512,128]{2,1,0:T(8,128)(2,1)S(1)} %bitcast.133, bf16[8,512,512]{2,1,0:T(8,128)(2,1)} %param.7), kind=kOutput, calls=%fused_computation.60 | convolution fusion | flops 536870912 | bytes 7340032 | tf_op jit(solution)/shard_map/bij,bjk->bik/dot_general | solution.py:35
  46.3 7.7 %fusion.38 = bf16[8,512,128]{1,2,0:T(8,128)(2,1)} fusion(bf16[1,8,512,512]{3,2,1,0:T(8,128)(2,1)} %param.6, bf16[8,512,128]{1,2,0:T(8,128)(2,1)S(1)} %copy.38, f32[8,128,512]{2,1,0:T(8,128)S(1)} %fusion.51, bf16[8,512,128]{2,1,0:T(8,128)(2,1)} %bitcast.140, bf16[8,512,512]{2,1,0:T(8,128)(2,1)} %param.8), kind=kOutput, calls=%fused_computation.29 | convolution fusion | flops 1076363264 | bytes 13631488 | tf_op jit(solution)/shard_map/bij,bjk->bik/dot_general | solution.py:41
  54.0 1.0 slice_bitcast_fusion.2
  55.0 5.0 %collective-permute-start.4 = (bf16[512,128]{0,1:T(8,128)(2,1)S(1)}, bf16[512,128]{0,1:T(8,128)(2,1)S(1)}, u32[]{:S(2)}, u32[]{:S(2)}) collective-permute-start(bf16[512,128]{0,1:T(8,128)(2,1)S(1)} %get-tuple-element.12), channel_id=1, source_target_pairs={{0,1},{1,2},{2,3},{3,4},{4,5},{5,6},{6,7},{8,9},{9,10},{10,11},{11... | collective-permute-start | bytes 393224 | tf_op jit(solution)/shard_map/ppermute | solution.py:16
  60.0 1.3 collective-permute-start.5
  61.3 1.6 copy.46
  62.9 0.1 copy.47
  63.0 0.2 collective-permute-done.5
  63.2 0.1 copy.49
  63.3 1.1 pad_maximum_fusion.2
  64.4 3.7 %fusion.52 = f32[8,128,512]{2,1,0:T(8,128)S(1)} fusion(bf16[8,512,128]{2,1,0:T(8,128)(2,1)S(1)} %bitcast.134, bf16[8,512,512]{2,1,0:T(8,128)(2,1)} %param.7), kind=kOutput, calls=%fused_computation.61 | convolution fusion | flops 536870912 | bytes 7340032 | tf_op jit(solution)/shard_map/bij,bjk->bik/dot_general | solution.py:35
  68.1 7.7 %fusion.35 = bf16[8,512,128]{1,2,0:T(8,128)(2,1)} fusion(bf16[1,8,512,512]{3,2,1,0:T(8,128)(2,1)} %param.6, bf16[8,512,128]{1,2,0:T(8,128)(2,1)S(1)} %copy.38, f32[8,128,512]{2,1,0:T(8,128)S(1)} %fusion.52, bf16[8,512,128]{2,1,0:T(8,128)(2,1)} %bitcast.141, bf16[8,512,512]{2,1,0:T(8,128)(2,1)} %param.8), kind=kOutput, calls=%fused_computation.28 | convolution fusion | flops 1076363264 | bytes 13631488 | tf_op jit(solution)/shard_map/bij,bjk->bik/dot_general | solution.py:41
  75.8 1.0 slice_bitcast_fusion
  76.8 5.0 %collective-permute-start.6 = (bf16[512,128]{0,1:T(8,128)(2,1)S(1)}, bf16[512,128]{0,1:T(8,128)(2,1)S(1)}, u32[]{:S(2)}, u32[]{:S(2)}) collective-permute-start(bf16[512,128]{0,1:T(8,128)(2,1)S(1)} %get-tuple-element.8), channel_id=1, source_target_pairs={{0,1},{1,2},{2,3},{3,4},{4,5},{5,6},{6,7},{8,9},{9,10},{10,11},{11... | collective-permute-start | bytes 393224 | tf_op jit(solution)/shard_map/ppermute | solution.py:16
  81.8 1.5 collective-permute-start.7
  83.9 1.6 copy.51
  85.5 0.1 copy.52
  85.7 0.1 copy.54
  85.8 1.1 pad_maximum_fusion
  86.9 3.7 %fusion.53 = f32[8,128,512]{2,1,0:T(8,128)S(1)} fusion(bf16[8,512,128]{2,1,0:T(8,128)(2,1)S(1)} %bitcast.135, bf16[8,512,512]{2,1,0:T(8,128)(2,1)} %param.7), kind=kOutput, calls=%fused_computation.62 | convolution fusion | flops 536870912 | bytes 7340032 | tf_op jit(solution)/shard_map/bij,bjk->bik/dot_general | solution.py:35
  90.6 8.0 %multiply_bitcast_fusion = f32[8,512,128]{1,2,0:T(8,128)} fusion(bf16[1,8,512,512]{3,2,1,0:T(8,128)(2,1)} %param.6, bf16[8,512,128]{1,2,0:T(8,128)(2,1)S(1)} %copy.38, f32[8,128,512]{2,1,0:T(8,128)S(1)} %fusion.53, bf16[8,512,128]{2,1,0:T(8,128)(2,1)} %bitcast.131, bf16[8,512,512]{2,1,0:T(8,128)(2,1)} %param.8, f32[]{:T(128)} %bitcast.129), kind=kOutput, calls=%fused_computation.22 | convolution fusion | flops 1077411840 | bytes 14680068 | tf_op jit(solution)/shard_map/bij,bjk->bik/dot_general | solution.py:41
  98.6 2.9 %copy.56 = f32[8,512,128]{2,1,0:T(8,128)} copy(f32[8,512,128]{1,2,0:T(8,128)} %multiply_bitcast_fusion) | data formatting | bytes 4194304 | tf_op jit(solution)/shard_map/mul | solution.py:44
  101.5 0.0 all-reduce.2.cloned.1.call-update
  101.5 71.9 %all-reduce.2.cloned.1.call-done = f32[4096,128]{1,0:T(8,128)} async-done(((f32[4096,128]{1,0:T(8,128)}), f32[4096,128]{1,0:T(8,128)}) %all-reduce.2.cloned.1.call-update) | async-done | bytes 2097168 | tf_op jit(solution)/shard_map/psum | solution.py:46
  173.4 5.7 %fusion.54 = f32[128,128]{1,0:T(8,128)S(1)} fusion(f32[4096,128]{1,0:T(8,128)} %all-reduce.2.cloned.1.call-done), kind=kOutput, calls=%fused_computation.63 | convolution fusion | flops 805306368 | bytes 2162688 | tf_op jit(solution)/shard_map/dot_general | solution.py:49
  179.1 15.0 %all-gather = f32[1024,128]{1,0:T(8,128)S(1)} all-gather(f32[128,128]{1,0:T(8,128)S(1)} %fusion.54), channel_id=2, replica_groups=mesh['pole'=4,'row'=8] {'row'}, dimensions={0}, use_global_device_ids=true | all-gather | bytes 589824 | tf_op jit(solution)/shard_map/all_gather | solution.py:50
  194.1 0.1 copy.57
  194.2 11.7 %cholesky.16 = f32[128,128]{1,0:T(8,128)S(1)} custom-call(f32[128,128]{1,0:T(8,128)S(1)} %fusion.48), custom_call_target="Cholesky" | custom-call | tf_op jit(solution)/shard_map/jit(cholesky)/cholesky | solution.py:52
  205.9 0.6 compare_reduce_fusion
  206.6 0.7 fusion.46
  207.3 9.8 %custom-call.7 = f32[1,128,128]{1,2,0:T(8,128)S(1)} custom-call(f32[1,128,128]{2,1,0:T(8,128)S(1)} %fusion.46), custom_call_target="InvertDiagBlocksLowerTriangular" | custom-call | tf_op jit(solution)/shard_map/jit(_solve_triangular)/triangular_solve | solution.py:53
  217.1 2.4 %fusion.44 = f32[1024,128]{1,0:T(8,128)} fusion(f32[4096,128]{1,0:T(8,128)} %all-reduce.2.cloned.1.call-done, s32[]{:T(128)S(6)} %select_n.7, f32[1,128,128]{1,2,0:T(8,128)S(1)} %custom-call.7), kind=kOutput, calls=%fused_computation.39 | convolution fusion | flops 201326592 | bytes 1114116 | tf_op jit(solution)/shard_map/jit(_solve_triangular)/triangular_solve | solution.py:53
  (12 shorter events, 0.1 us)
Async XLA Ops:
  6.5 166.9 %all-reduce.2.cloned.1.call-start = ((), (), s32[]{:S(2)}) async-start(), calls=%async_computation | async-start | bytes 4194304 | tf_op jit(solution)/shard_map/psum | solution.py:46
  6.5 7.6 %copy-start = (bf16[4096,128]{1,0:T(8,128)(2,1)S(1)}, bf16[4096,128]{1,0:T(8,128)(2,1)}, u32[]{:S(2)}) copy-start(bf16[4096,128]{1,0:T(8,128)(2,1)} %param.5) | copy-start | bytes 3145732
  10.4 4.3 %collective-permute-start = (bf16[512,128]{1,0:T(8,128)(2,1)S(1)}, bf16[512,128]{1,0:T(8,128)(2,1)S(1)}, u32[]{:S(2)}, u32[]{:S(2)}) collective-permute-start(bf16[512,128]{1,0:T(8,128)(2,1)S(1)} %get-tuple-element.20), channel_id=1, source_target_pairs={{0,1},{1,2},{2,3},{3,4},{4,5},{5,6},{6,7},{8,9},{9,10},{10,11},{11... | collective-permute-start | bytes 393224 | tf_op jit(solution)/shard_map/ppermute | solution.py:16
  12.8 5.5 %collective-permute-start.1 = (bf16[512,128]{1,0:T(8,128)(2,1)S(1)}, bf16[512,128]{1,0:T(8,128)(2,1)}, u32[]{:S(2)}, u32[]{:S(2)}) collective-permute-start(bf16[512,128]{1,0:T(8,128)(2,1)S(1)} %get-tuple-element.19), channel_id=1, source_target_pairs={{1,0},{2,1},{3,2},{4,3},{5,4},{6,5},{7,6},{9,8},{10,9},{11,10},{12... | collective-permute-start | bytes 393224 | tf_op jit(solution)/shard_map/ppermute | solution.py:17
  32.7 8.4 %collective-permute-start.2 = (bf16[512,128]{0,1:T(8,128)(2,1)S(1)}, bf16[512,128]{0,1:T(8,128)(2,1)S(1)}, u32[]{:S(2)}, u32[]{:S(2)}) collective-permute-start(bf16[512,128]{0,1:T(8,128)(2,1)S(1)} %get-tuple-element.16), channel_id=1, source_target_pairs={{0,1},{1,2},{2,3},{3,4},{4,5},{5,6},{6,7},{8,9},{9,10},{10,11},{11... | collective-permute-start | bytes 393224 | tf_op jit(solution)/shard_map/ppermute | solution.py:16
  38.2 3.2 %collective-permute-start.3 = (bf16[512,128]{0,1:T(8,128)(2,1)S(1)}, bf16[512,128]{0,1:T(8,128)(2,1)S(1)}, u32[]{:S(2)}, u32[]{:S(2)}) collective-permute-start(bf16[512,128]{0,1:T(8,128)(2,1)S(1)} %get-tuple-element.15), channel_id=1, source_target_pairs={{1,0},{2,1},{3,2},{4,3},{5,4},{6,5},{7,6},{9,8},{10,9},{11,10},{12... | collective-permute-start | bytes 393224 | tf_op jit(solution)/shard_map/ppermute | solution.py:17
  55.0 7.9 %collective-permute-start.4 = (bf16[512,128]{0,1:T(8,128)(2,1)S(1)}, bf16[512,128]{0,1:T(8,128)(2,1)S(1)}, u32[]{:S(2)}, u32[]{:S(2)}) collective-permute-start(bf16[512,128]{0,1:T(8,128)(2,1)S(1)} %get-tuple-element.12), channel_id=1, source_target_pairs={{0,1},{1,2},{2,3},{3,4},{4,5},{5,6},{6,7},{8,9},{9,10},{10,11},{11... | collective-permute-start | bytes 393224 | tf_op jit(solution)/shard_map/ppermute | solution.py:16
  60.0 3.2 %collective-permute-start.5 = (bf16[512,128]{0,1:T(8,128)(2,1)S(1)}, bf16[512,128]{0,1:T(8,128)(2,1)S(1)}, u32[]{:S(2)}, u32[]{:S(2)}) collective-permute-start(bf16[512,128]{0,1:T(8,128)(2,1)S(1)} %get-tuple-element.11), channel_id=1, source_target_pairs={{1,0},{2,1},{3,2},{4,3},{5,4},{6,5},{7,6},{9,8},{10,9},{11,10},{12... | collective-permute-start | bytes 393224 | tf_op jit(solution)/shard_map/ppermute | solution.py:17
  76.8 8.7 %collective-permute-start.6 = (bf16[512,128]{0,1:T(8,128)(2,1)S(1)}, bf16[512,128]{0,1:T(8,128)(2,1)S(1)}, u32[]{:S(2)}, u32[]{:S(2)}) collective-permute-start(bf16[512,128]{0,1:T(8,128)(2,1)S(1)} %get-tuple-element.8), channel_id=1, source_target_pairs={{0,1},{1,2},{2,3},{3,4},{4,5},{5,6},{6,7},{8,9},{9,10},{10,11},{11... | collective-permute-start | bytes 393224 | tf_op jit(solution)/shard_map/ppermute | solution.py:16
  81.8 3.9 %collective-permute-start.7 = (bf16[512,128]{0,1:T(8,128)(2,1)S(1)}, bf16[512,128]{0,1:T(8,128)(2,1)S(1)}, u32[]{:S(2)}, u32[]{:S(2)}) collective-permute-start(bf16[512,128]{0,1:T(8,128)(2,1)S(1)} %get-tuple-element.7), channel_id=1, source_target_pairs={{1,0},{2,1},{3,2},{4,3},{5,4},{6,5},{7,6},{9,8},{10,9},{11,10},{12... | collective-permute-start | bytes 393224 | tf_op jit(solution)/shard_map/ppermute | solution.py:17
Sparse Core Ops, SparseCore 0:
  101.6 71.7 all-reduce.1
